TPU v7x, 32 devices: a whole 2x2x4 slice. The times are simulated.
32 devices in a mesh: section: 2 (over core), ctx: 4 (over y, x), tp: 4 (over z).
Axes of the slice: x: 2, y: 2, z: 4, core: 2. Of those that a mesh axis runs over, the one named last changes fastest.
Arguments:
- inputs: bfloat16 [4, 1024, 2048], P(None, ('ctx', 'tp')), may hold values from -6 to 6
- segments: int32 [4, 1024], replicated, may hold values from 0 to 3, never falling along the last dimension, each value on 1 to 512 neighbouring positions
- cotangent: bfloat16 [4, 1024, 2048], P(None, ('ctx', 'tp')), may hold values from -6 to 6
- ln_gain: bfloat16 [2, 2048], P('section'), may hold values from 0.5 to 1.5
- ln_bias: bfloat16 [2, 2048], P('section'), may hold values from -3 to 3
- qkv_weight: bfloat16 [2, 3, 2048, 2048], P('section', None, None, 'tp'), may hold values from -1 to 1, as said below
- qkv_bias: bfloat16 [2, 3, 2048], P('section', None, 'tp'), may hold values from -3 to 3
- dense_weight: bfloat16 [2, 2048, 2048], P('section', 'tp'), may hold values from -0.75 to 0.75
- fc1_weight: bfloat16 [2, 2048, 8192], P('section', None, 'tp'), may hold values from -0.125 to 0.125
- fc1_bias: bfloat16 [2, 8192], P('section', 'tp'), may hold values from -3 to 3
- fc2_weight: bfloat16 [2, 8192, 2048], P('section', 'tp'), may hold values from -0.0625 to 0.0625
- out_bias: bfloat16 [2, 2048], P('section'), may hold values from -3 to 3
Outputs:
- layer_outputs: bfloat16 [2, 4, 1024, 2048], P('section', None, ('ctx', 'tp'))
- input_grads: bfloat16 [2, 4, 1024, 2048], P('section', None, ('ctx', 'tp'))
- ln_gain_grad: float32 [2, 2048], P('section')
- ln_bias_grad: float32 [2, 2048], P('section')
- qkv_weight_grad: float32 [2, 3, 2048, 2048], P('section', None, None, 'tp')
- qkv_bias_grad: float32 [2, 3, 2048], P('section', None, 'tp')
- dense_weight_grad: float32 [2, 2048, 2048], P('section', 'tp')
- fc1_weight_grad: float32 [2, 2048, 8192], P('section', None, 'tp')
- fc1_bias_grad: float32 [2, 8192], P('section', 'tp')
- fc2_weight_grad: float32 [2, 8192, 2048], P('section', 'tp')
- out_bias_grad: float32 [2, 2048], P('section')
Inputs may be any that keep to these rules, and one draw needn't show every extreme that they name: `segments`: within a sequence the ids never fall; each of the 4 documents has 1 to 512 tokens, one exactly 512. `qkv_weight`: entries of order 2048^(-1/2).
All inputs are finite; a program needn't handle non-finite values.
Results may differ from a plain program's by a relative error of at most 0.02.
Values may be sent and summed in bfloat16 or wider, within the bound.
No kernel may reach another device: no remote copies, remote signals or barrier semaphores. Data moves between devices by JAX's collectives and lax.ppermute only.
A program may use at most 640 MiB of HBM per device.

v0:
```python
import jax
import jax.numpy as jnp
from jax import lax
from jax.sharding import PartitionSpec as P

HEAD = 64
ROT = 32
EPSILON = 1e-05
NEGATIVE = -1e30
GELU_ROOT = 0.7978845608028654
GELU_CUBE = 0.044715


def from_behind(x, axis, by):
    length = lax.axis_size(axis)
    pairs = [(i, i + by) for i in range(length) if 0 <= i + by < length]
    return lax.ppermute(x, axis, pairs)


def rope_tables(positions, rot_dims):
    half_dims = rot_dims // 2
    frequency = 10000.0 ** (-(2.0 * jnp.arange(half_dims, dtype=jnp.float32)) / rot_dims)
    angles = positions.astype(jnp.float32)[:, None] * frequency[None, :]
    return (jnp.cos(angles)[:, None, :], jnp.sin(angles)[:, None, :])


def rotate(values_in, cosine, sine, rot_dims):
    half_dims = rot_dims // 2
    lower_half = values_in[..., :half_dims]
    upper_half = values_in[..., half_dims:rot_dims]
    return jnp.concatenate(
        [
            lower_half * cosine - upper_half * sine,
            upper_half * cosine + lower_half * sine,
            values_in[..., rot_dims:],
        ],
        axis=-1,
    )


def unrotate(grads_in, cosine, sine, rot_dims):
    half_dims = rot_dims // 2
    lower_half = grads_in[..., :half_dims]
    upper_half = grads_in[..., half_dims:rot_dims]
    return jnp.concatenate(
        [
            lower_half * cosine + upper_half * sine,
            upper_half * cosine - lower_half * sine,
            grads_in[..., rot_dims:],
        ],
        axis=-1,
    )


def gelu_slope(pre_act):
    tangent = jnp.tanh(GELU_ROOT * (pre_act + GELU_CUBE * pre_act * pre_act * pre_act))
    return 0.5 * (1.0 + tangent) + 0.5 * pre_act * (1.0 - tangent * tangent) * GELU_ROOT * (
        1.0 + 3.0 * GELU_CUBE * pre_act * pre_act
    )


def normalize(x_rows):
    centered = x_rows - jnp.mean(x_rows, axis=1, keepdims=True)
    inv_std = lax.rsqrt(jnp.mean(centered * centered, axis=1, keepdims=True) + EPSILON)
    return (centered * inv_std, inv_std)


def take_slot(buffer, slot_index):
    return lax.dynamic_index_in_dim(buffer, slot_index, 0, keepdims=False)


def put_slot(buffer, slot_index, leaf_value, active):
    return lax.dynamic_update_index_in_dim(
        buffer, jnp.where(active, leaf_value, take_slot(buffer, slot_index)), slot_index, 0
    )


def on_device(
    inputs,
    segments,
    cotangent,
    ln_gain,
    ln_bias,
    qkv_weight,
    qkv_bias,
    dense_weight,
    fc1_weight,
    fc1_bias,
    fc2_weight,
    out_bias,
):
    sections = lax.axis_size("section")
    section_id = lax.axis_index("section")
    ctx_id = lax.axis_index("ctx")
    batches, row_count, model_width = inputs.shape
    ctx_rows = row_count * lax.axis_size("tp")
    total_rows = ctx_rows * lax.axis_size("ctx")
    local_dim = qkv_weight.shape[3]
    heads_local = local_dim // HEAD
    score_scale = HEAD ** (-0.5)
    gain_vec = ln_gain[0].astype(jnp.float32)
    shift_vec = ln_bias[0].astype(jnp.float32)
    w_in = jnp.concatenate(
        [qkv_weight[0, 0], qkv_weight[0, 1], qkv_weight[0, 2], fc1_weight[0]], axis=1
    )
    bias_in = jnp.concatenate([qkv_bias[0].reshape(-1), fc1_bias[0]]).astype(jnp.float32)
    w_out = jnp.concatenate([dense_weight[0], fc2_weight[0]], axis=0)
    bias_vec = out_bias[0].astype(jnp.float32)
    query_pos = ctx_id * ctx_rows + jnp.arange(ctx_rows, dtype=jnp.int32)
    cosine, sine = rope_tables(query_pos, ROT)
    key_pos = jnp.arange(total_rows, dtype=jnp.int32)
    contract_rows = (((0,), (0,)), ((), ()))
    contract_cols = (((1,), (1,)), ((), ()))
    received = jnp.zeros((row_count, model_width), jnp.bfloat16)
    layer_out = jnp.zeros((batches, row_count, model_width), jnp.bfloat16)
    buffers = None
    for clock_tick in range(batches + sections - 1):
        micro_batch = clock_tick - section_id
        active = (micro_batch >= 0) & (micro_batch < batches)
        slot_index = jnp.clip(micro_batch, 0, batches - 1)
        x_rows = jnp.where(section_id == 0, take_slot(inputs, slot_index), received).astype(
            jnp.float32
        )
        doc_all = take_slot(segments, slot_index)
        normalized, inv_std = normalize(x_rows)
        normed_b = (normalized * gain_vec + shift_vec).astype(jnp.bfloat16)
        doc_rows = lax.dynamic_slice_in_dim(doc_all, ctx_id * ctx_rows, ctx_rows)
        stored = {}
        projected = jnp.dot(
            lax.all_gather(normed_b, "tp", axis=0, tiled=True),
            w_in,
            preferred_element_type=jnp.float32,
        )
        projected = projected + bias_in
        query_pre = projected[:, :local_dim].reshape(ctx_rows, heads_local, HEAD)
        key_pre = projected[:, local_dim : 2 * local_dim].reshape(ctx_rows, heads_local, HEAD)
        queries_b = rotate(query_pre, cosine, sine, ROT).astype(jnp.bfloat16)
        keys_b = rotate(key_pre, cosine, sine, ROT).astype(jnp.bfloat16)
        values_b = (
            projected[:, 2 * local_dim : 3 * local_dim]
            .reshape(ctx_rows, heads_local, HEAD)
            .astype(jnp.bfloat16)
        )
        up_pre = projected[:, 3 * local_dim :]
        run_max = jnp.full((heads_local, ctx_rows), NEGATIVE, jnp.float32)
        keys_part = lax.all_gather(keys_b, "ctx", axis=0, tiled=True)
        values_part = lax.all_gather(values_b, "ctx", axis=0, tiled=True)
        part_rows = keys_part.shape[0]
        part_pos = jnp.arange(part_rows, dtype=jnp.int32)
        allowed = (part_pos[None, :] <= query_pos[:, None]) & (
            doc_all[None, :] == doc_rows[:, None]
        )
        scores = (
            jnp.einsum("qhd,khd->hqk", queries_b, keys_part, preferred_element_type=jnp.float32)
            * score_scale
        )
        scores = jnp.where(allowed[None], scores, NEGATIVE)
        new_max = jnp.maximum(run_max, jnp.max(scores, axis=2))
        weights = jnp.where(allowed[None], jnp.exp(scores - new_max[:, :, None]), 0.0)
        run_sum = jnp.sum(weights, axis=2)
        accumulated = jnp.einsum(
            "hqk,khd->hqd",
            weights.astype(jnp.bfloat16),
            values_part,
            preferred_element_type=jnp.float32,
        )
        run_max, run_sum, accumulated = (new_max, run_sum, accumulated)
        attended = jnp.transpose(accumulated / run_sum[:, :, None], (1, 0, 2))
        log_total = run_max + jnp.log(run_sum)
        attended_b = attended.reshape(ctx_rows, local_dim).astype(jnp.bfloat16)
        gelu_b = jax.nn.gelu(up_pre, approximate=True).astype(jnp.bfloat16)
        branch_in = jnp.concatenate([attended_b, gelu_b], axis=1)
        branch = lax.psum_scatter(
            jnp.dot(branch_in, w_out, preferred_element_type=jnp.float32).astype(jnp.bfloat16),
            "tp",
            scatter_dimension=0,
            tiled=True,
        ).astype(jnp.float32)
        result = x_rows + branch + bias_vec
        stored["x_rows"] = x_rows.astype(jnp.bfloat16)
        stored["queries"] = queries_b
        stored["keys"] = keys_b
        stored["values"] = values_b
        stored["up_pre"] = up_pre
        stored["branch_in"] = branch_in
        stored["attended"] = attended
        stored["log_total"] = log_total
        result, stored = (result, stored)
        result_b = result.astype(jnp.bfloat16)
        if buffers is None:
            buffers = jax.tree.map(
                lambda leaf_value: jnp.zeros((batches,) + leaf_value.shape, leaf_value.dtype),
                stored,
            )
        buffers = jax.tree.map(
            lambda buffer, leaf_value: put_slot(buffer, slot_index, leaf_value, active),
            buffers,
            stored,
        )
        layer_out = put_slot(layer_out, slot_index, result_b, active)
        received = from_behind(result_b, "section", 1)
    received = jnp.zeros((row_count, model_width), jnp.bfloat16)
    grad_inputs = jnp.zeros((batches, row_count, model_width), jnp.bfloat16)
    totals = None
    for clock_tick in range(batches + sections - 1):
        micro_batch = clock_tick - (sections - 1 - section_id)
        active = (micro_batch >= 0) & (micro_batch < batches)
        slot_index = jnp.clip(micro_batch, 0, batches - 1)
        grad_out = jnp.where(
            section_id == sections - 1, take_slot(cotangent, slot_index), received
        ).astype(jnp.float32)
        stored = jax.tree.map(lambda buffer: take_slot(buffer, slot_index), buffers)
        doc_all = take_slot(segments, slot_index)
        backward_normalized, backward_inv_std = normalize(stored["x_rows"].astype(jnp.float32))
        backward_normed_b = (backward_normalized * gain_vec + shift_vec).astype(jnp.bfloat16)
        backward_doc_rows = lax.dynamic_slice_in_dim(doc_all, ctx_id * ctx_rows, ctx_rows)
        backward_branch_in = stored["branch_in"]
        grad_out_b = grad_out.astype(jnp.bfloat16)
        fold_pieces = lax.all_gather(grad_out_b, "tp", axis=0, tiled=True)
        grad_w = lax.dot_general(
            backward_branch_in, fold_pieces, contract_rows, preferred_element_type=jnp.float32
        )
        grad_rows = lax.dot_general(
            fold_pieces, w_out, contract_cols, preferred_element_type=jnp.float32
        )
        grad_attn_b = (
            grad_rows[:, :local_dim].astype(jnp.bfloat16).reshape(ctx_rows, heads_local, HEAD)
        )
        grad_up = grad_rows[:, local_dim:] * gelu_slope(stored["up_pre"])
        row_delta = jnp.transpose(
            jnp.sum(grad_attn_b.astype(jnp.float32) * stored["attended"], axis=2)
        )
        keys_all = lax.all_gather(stored["keys"], "ctx", axis=0, tiled=True)
        values_all = lax.all_gather(stored["values"], "ctx", axis=0, tiled=True)
        backward_queries_b = stored["queries"]
        backward_allowed = (key_pos[None, :] <= query_pos[:, None]) & (
            doc_all[None, :] == backward_doc_rows[:, None]
        )
        backward_scores = (
            jnp.einsum(
                "qhd,khd->hqk", backward_queries_b, keys_all, preferred_element_type=jnp.float32
            )
            * score_scale
        )
        probs = jnp.where(
            backward_allowed[None], jnp.exp(backward_scores - stored["log_total"][:, :, None]), 0.0
        )
        grad_probs = jnp.einsum(
            "qhd,khd->hqk", grad_attn_b, values_all, preferred_element_type=jnp.float32
        )
        grad_scores_b = (probs * (grad_probs - row_delta[:, :, None])).astype(jnp.bfloat16)
        grad_query = (
            jnp.einsum("hqk,khd->qhd", grad_scores_b, keys_all, preferred_element_type=jnp.float32)
            * score_scale
        )
        probs_b = probs.astype(jnp.bfloat16)
        grad_key_part = (
            jnp.einsum(
                "hqk,qhd->khd",
                grad_scores_b,
                backward_queries_b,
                preferred_element_type=jnp.float32,
            )
            * score_scale
        )
        grad_value_part = jnp.einsum(
            "hqk,qhd->khd", probs_b, grad_attn_b, preferred_element_type=jnp.float32
        )
        key_grads = (
            lax.psum_scatter(
                jnp.concatenate([grad_key_part, grad_value_part], axis=2)
                .reshape(ctx_rows * lax.axis_size("ctx"), 2 * local_dim)
                .astype(jnp.bfloat16),
                "ctx",
                scatter_dimension=0,
                tiled=True,
            )
            .astype(jnp.float32)
            .reshape(ctx_rows, heads_local, 2 * HEAD)
        )
        grad_key_raw = key_grads[..., :HEAD]
        grad_value = key_grads[..., HEAD:]
        grad_key = unrotate(grad_key_raw, cosine, sine, ROT)
        grad_query = unrotate(grad_query, cosine, sine, ROT)
        grad_proj_b = jnp.concatenate(
            [
                grad_query.reshape(ctx_rows, local_dim),
                grad_key.reshape(ctx_rows, local_dim),
                grad_value.reshape(ctx_rows, local_dim),
                grad_up,
            ],
            axis=1,
        ).astype(jnp.bfloat16)
        grad_bias_in = jnp.sum(grad_proj_b.astype(jnp.float32), axis=0)
        grad_w_in = lax.dot_general(
            lax.all_gather(backward_normed_b, "tp", axis=0, tiled=True),
            grad_proj_b,
            contract_rows,
            preferred_element_type=jnp.float32,
        )
        grad_normed = lax.psum_scatter(
            lax.dot_general(
                grad_proj_b, w_in, contract_cols, preferred_element_type=jnp.float32
            ).astype(jnp.bfloat16),
            "tp",
            scatter_dimension=0,
            tiled=True,
        ).astype(jnp.float32)
        grad_gain = jnp.sum(grad_normed * backward_normalized, axis=0)
        grad_shift = jnp.sum(grad_normed, axis=0)
        scaled = grad_normed * gain_vec
        grad_x = grad_out + backward_inv_std * (
            scaled
            - jnp.mean(scaled, axis=1, keepdims=True)
            - backward_normalized * jnp.mean(scaled * backward_normalized, axis=1, keepdims=True)
        )
        grad_x, terms = (
            grad_x,
            (grad_w_in, grad_w, grad_bias_in, grad_gain, grad_shift, jnp.sum(grad_out, axis=0)),
        )
        terms = tuple((jnp.where(active, term_value, 0.0) for term_value in terms))
        totals = terms if totals is None else jax.tree.map(jnp.add, totals, terms)
        grad_x_b = grad_x.astype(jnp.bfloat16)
        grad_inputs = put_slot(grad_inputs, slot_index, grad_x_b, active)
        received = from_behind(grad_x_b, "section", -1)
    total_w_in, total_w_out, total_bias_in, total_gain, total_shift, total_bias_out = totals
    sum_w_in, sum_w_out, sum_bias_in, sum_gain, sum_shift, sum_bias_out = (
        lax.psum(total_w_in.astype(jnp.bfloat16), "ctx").astype(jnp.float32),
        lax.psum(total_w_out.astype(jnp.bfloat16), "ctx").astype(jnp.float32),
        lax.psum(total_bias_in.astype(jnp.bfloat16), "ctx").astype(jnp.float32),
        lax.psum(total_gain.astype(jnp.bfloat16), "ctx").astype(jnp.float32),
        lax.psum(total_shift.astype(jnp.bfloat16), "ctx").astype(jnp.float32),
        lax.psum(total_bias_out.astype(jnp.bfloat16), "ctx").astype(jnp.float32),
    )
    sum_gain, sum_shift, sum_bias_out = lax.psum((sum_gain, sum_shift, sum_bias_out), "tp")
    qkv_grad = jnp.transpose(
        sum_w_in[:, : 3 * local_dim].reshape(model_width, 3, local_dim), (1, 0, 2)
    )
    return (
        layer_out[None],
        grad_inputs[None],
        sum_gain[None],
        sum_shift[None],
        qkv_grad[None],
        sum_bias_in[: 3 * local_dim].reshape(3, local_dim)[None],
        sum_w_out[:local_dim][None],
        sum_w_in[:, 3 * local_dim :][None],
        sum_bias_in[3 * local_dim :][None],
        sum_w_out[local_dim:][None],
        sum_bias_out[None],
    )


def solution(mesh):
    return jax.shard_map(
        on_device,
        mesh=mesh,
        in_specs=(
            P(None, ("ctx", "tp"), None),
            P(),
            P(None, ("ctx", "tp"), None),
            P("section", None),
            P("section", None),
            P("section", None, None, "tp"),
            P("section", None, "tp"),
            P("section", "tp", None),
            P("section", None, "tp"),
            P("section", "tp"),
            P("section", "tp", None),
            P("section", None),
        ),
        out_specs=(
            P("section", None, ("ctx", "tp"), None),
            P("section", None, ("ctx", "tp"), None),
            P("section", None),
            P("section", None),
            P("section", None, None, "tp"),
            P("section", None, "tp"),
            P("section", "tp", None),
            P("section", None, "tp"),
            P("section", "tp"),
            P("section", "tp", None),
            P("section", None),
        ),
        check_vma=False,
    )
```

profile of v0, /device:TPU:0, one launch (start us, length us, event | category | flops | bytes accessed | tf_op | source)
XLA Modules:
  0.0 2298.0 jit_solution(12967685389564836496)
XLA Ops:
  19.1 12.1 pad_maximum_fusion
  31.2 12.5 all-gather.47.cloned.1.call-done
  62.0 18.5 all-gather.49.cloned.1.call-done
  89.4 19.9 all-gather.51.cloned.1.call-done
  124.1 27.4 %reduce-scatter.16.cloned.1.call-done = bf16[64,2048]{1,0:T(8,128)(2,1)} async-done(((bf16[256,2048]{1,0:T(8,128)(2,1)}), bf16[64,2048]{1,0:T(8,128)(2,1)}) %reduce-scatter.16.cloned.1.call-update) | async-done | bytes 262160 | tf_op jit(solution)/shard_map/reduce_scatter | solution.py:173
  156.8 27.9 %all-gather.53.cloned.1.call-done = bf16[256,2048]{1,0:T(8,128)(2,1)} async-done(((bf16[64,2048]{1,0:T(8,128)(2,1)}), bf16[256,2048]{1,0:T(8,128)(2,1)}) %all-gather.53.cloned.1.call-update) | async-done | bytes 1048592 | tf_op jit(solution)/shard_map/all_gather | solution.py:130
  215.8 13.5 all-gather.55.cloned.1.call-done
  238.3 19.2 all-gather.57.cloned.1.call-done
  275.1 26.7 %reduce-scatter.18.cloned.1.call-done = bf16[64,2048]{1,0:T(8,128)(2,1)} async-done(((bf16[256,2048]{1,0:T(8,128)(2,1)}), bf16[64,2048]{1,0:T(8,128)(2,1)}) %reduce-scatter.18.cloned.1.call-update) | async-done | bytes 262160 | tf_op jit(solution)/shard_map/reduce_scatter | solution.py:173
  308.2 27.7 %all-gather.59.cloned.1.call-done = bf16[256,2048]{1,0:T(8,128)(2,1)} async-done(((bf16[64,2048]{1,0:T(8,128)(2,1)}), bf16[256,2048]{1,0:T(8,128)(2,1)}) %all-gather.59.cloned.1.call-update) | async-done | bytes 1048592 | tf_op jit(solution)/shard_map/all_gather | solution.py:130
  363.1 17.4 all-gather.61.cloned.1.call-done
  389.5 19.2 all-gather.63.cloned.1.call-done
  426.3 26.7 %reduce-scatter.20.cloned.1.call-done = bf16[64,2048]{1,0:T(8,128)(2,1)} async-done(((bf16[256,2048]{1,0:T(8,128)(2,1)}), bf16[64,2048]{1,0:T(8,128)(2,1)}) %reduce-scatter.20.cloned.1.call-update) | async-done | bytes 262160 | tf_op jit(solution)/shard_map/reduce_scatter | solution.py:173
  459.6 27.5 %all-gather.65.cloned.1.call-done = bf16[256,2048]{1,0:T(8,128)(2,1)} async-done(((bf16[64,2048]{1,0:T(8,128)(2,1)}), bf16[256,2048]{1,0:T(8,128)(2,1)}) %all-gather.65.cloned.1.call-update) | async-done | bytes 1048592 | tf_op jit(solution)/shard_map/all_gather | solution.py:130
  516.7 14.9 all-gather.67.cloned.1.call-done
  540.7 19.0 all-gather.69.cloned.1.call-done
  598.6 19.9 reduce-scatter.22.cloned.1.call-done
  732.7 20.9 all-gather.95.cloned.1.call-done
  762.5 19.2 all-gather.99.cloned.1.call-done
  853.4 26.6 %reduce-scatter.28.cloned.1.call-done = bf16[64,2048]{1,0:T(8,128)(2,1)} async-done(((bf16[256,2048]{1,0:T(8,128)(2,1)}), bf16[64,2048]{1,0:T(8,128)(2,1)}) %reduce-scatter.28.cloned.1.call-update) | async-done | bytes 262160 | tf_op jit(solution)/shard_map/reduce_scatter | solution.py:301
  892.1 14.6 all-gather.101.cloned.1.call-done
  912.8 23.4 %all-gather.77.cloned.1.call-done = bf16[256,2048]{1,0:T(8,128)(2,1)} async-done(((bf16[64,2048]{1,0:T(8,128)(2,1)}), bf16[256,2048]{1,0:T(8,128)(2,1)}) %all-gather.77.cloned.1.call-update) | async-done | bytes 1048592 | tf_op jit(solution)/shard_map/all_gather | solution.py:219
  983.3 25.3 %reduce-scatter.30.cloned.1.call-done = bf16[256,1024]{0,1:T(8,128)(2,1)} async-done(((bf16[1024,1024]{0,1:T(8,128)(2,1)}), bf16[256,1024]{0,1:T(8,128)(2,1)}) %reduce-scatter.30.cloned.1.call-update) | async-done | bytes 524304 | tf_op jit(solution)/shard_map/reduce_scatter | solution.py:270
  1036.9 25.0 %reduce-scatter.32.cloned.1.call-done = bf16[64,2048]{1,0:T(8,128)(2,1)} async-done(((bf16[256,2048]{1,0:T(8,128)(2,1)}), bf16[64,2048]{1,0:T(8,128)(2,1)}) %reduce-scatter.32.cloned.1.call-update) | async-done | bytes 262160 | tf_op jit(solution)/shard_map/reduce_scatter | solution.py:301
  1074.3 14.3 all-gather.105.cloned.1.call-done
  1094.5 23.6 %all-gather.79.cloned.1.call-done = bf16[256,2048]{1,0:T(8,128)(2,1)} async-done(((bf16[64,2048]{1,0:T(8,128)(2,1)}), bf16[256,2048]{1,0:T(8,128)(2,1)}) %all-gather.79.cloned.1.call-update) | async-done | bytes 1048592 | tf_op jit(solution)/shard_map/all_gather | solution.py:219
  1165.6 25.3 %reduce-scatter.34.cloned.1.call-done = bf16[256,1024]{0,1:T(8,128)(2,1)} async-done(((bf16[1024,1024]{0,1:T(8,128)(2,1)}), bf16[256,1024]{0,1:T(8,128)(2,1)}) %reduce-scatter.34.cloned.1.call-update) | async-done | bytes 524304 | tf_op jit(solution)/shard_map/reduce_scatter | solution.py:270
  1219.8 25.0 %reduce-scatter.36.cloned.1.call-done = bf16[64,2048]{1,0:T(8,128)(2,1)} async-done(((bf16[256,2048]{1,0:T(8,128)(2,1)}), bf16[64,2048]{1,0:T(8,128)(2,1)}) %reduce-scatter.36.cloned.1.call-update) | async-done | bytes 262160 | tf_op jit(solution)/shard_map/reduce_scatter | solution.py:301
  1255.8 15.8 all-gather.109.cloned.1.call-done
  1277.5 23.4 %all-gather.81.cloned.1.call-done = bf16[256,2048]{1,0:T(8,128)(2,1)} async-done(((bf16[64,2048]{1,0:T(8,128)(2,1)}), bf16[256,2048]{1,0:T(8,128)(2,1)}) %all-gather.81.cloned.1.call-update) | async-done | bytes 1048592 | tf_op jit(solution)/shard_map/all_gather | solution.py:219
  1348.1 25.4 %reduce-scatter.38.cloned.1.call-done = bf16[256,1024]{0,1:T(8,128)(2,1)} async-done(((bf16[1024,1024]{0,1:T(8,128)(2,1)}), bf16[256,1024]{0,1:T(8,128)(2,1)}) %reduce-scatter.38.cloned.1.call-update) | async-done | bytes 524304 | tf_op jit(solution)/shard_map/reduce_scatter | solution.py:270
  1402.5 25.0 %reduce-scatter.40.cloned.1.call-done = bf16[64,2048]{1,0:T(8,128)(2,1)} async-done(((bf16[256,2048]{1,0:T(8,128)(2,1)}), bf16[64,2048]{1,0:T(8,128)(2,1)}) %reduce-scatter.40.cloned.1.call-update) | async-done | bytes 262160 | tf_op jit(solution)/shard_map/reduce_scatter | solution.py:301
  1440.0 14.2 all-gather.113.cloned.1.call-done
  1460.5 23.3 %all-gather.83.cloned.1.call-done = bf16[256,2048]{1,0:T(8,128)(2,1)} async-done(((bf16[64,2048]{1,0:T(8,128)(2,1)}), bf16[256,2048]{1,0:T(8,128)(2,1)}) %all-gather.83.cloned.1.call-update) | async-done | bytes 1048592 | tf_op jit(solution)/shard_map/all_gather | solution.py:219
  1492.0 19.4 all-gather.115.cloned.1.call-done
  1580.5 15.2 fusion.526
  1595.8 13.7 fusion.527
  1619.7 13.6 fusion.525
  1643.6 15.6 fusion.524
  1661.5 26.5 %add_convert_fusion.1 = bf16[2560,2048]{1,0:T(8,128)(2,1)} fusion(f32[2560,2048]{1,0:T(8,128)} %fusion.191, f32[2560,2048]{1,0:T(8,128)} %fusion.193, f32[2560,2048]{1,0:T(8,128)} %fusion.195, f32[2560,2048]{1,0:T(8,128)} %fusion.197, bf16[256,2048]{1,0:T(8,128)(2,1)} %all-gather.83.cloned.1.call-done, pred[]{:T(512)S(6)} %and.120, pred[]{:T(512)S(6)} %and.118, ...), kind=kOutput, calls=%fused_computation.1 | convolution fusion | flops 2736783360 | bytes 96731144 | tf_op jit(solution)/shard_map/dot_general | solution.py:220
  1711.5 35.0 %add_convert_fusion = bf16[2048,3584]{1,0:T(8,128)(2,1)} fusion(f32[2048,3584]{1,0:T(8,128)} %fusion.524, f32[2048,3584]{1,0:T(8,128)} %fusion.525, f32[2048,3584]{1,0:T(8,128)} %fusion.526, f32[2048,3584]{1,0:T(8,128)} %fusion.527, bf16[256,2048]{1,0:T(8,128)(2,1)} %all-gather.93.cloned.1.call-done, pred[]{:T(512)S(6)} %and.120, pred[]{:T(512)S(6)} %and.118, ...), kind=kOutput, calls=%fused_computation | convolution fusion | flops 3838836736 | bytes 135004160 | tf_op jit(solution)/shard_map/dot_general | solution.py:295
  1758.1 16.3 all-reduce.1
  1775.6 19.8 all-reduce
  1796.9 407.8 %all-reduce.5.cloned.1.call-done = (bf16[2048,3584]{1,0:T(8,128)(2,1)}, bf16[2560,2048]{1,0:T(8,128)(2,1)}) async-done(((bf16[2048,3584]{1,0:T(8,128)(2,1)}, bf16[2560,2048]{1,0:T(8,128)(2,1)}), (bf16[2048,3584]{1,0:T(8,128)(2,1)}, bf16[2560,2048]{1,0:T(8,128)(2,1)})) %all-reduce.5.cloned.1.call-update) | async-done | bytes 25165840 | tf_op jit(solution)/shard_map/psum | solution.py:328
  2226.0 13.8 convert_element_type.735
  2244.5 12.6 copy.144
  2257.1 12.6 copy.150
  2269.7 21.2 slice_bitcast_fusion
  (889 shorter events, 916.8 us)
Async XLA Ops:
  12.8 67.7 %all-gather.49.cloned.1.call-start = ((), (), s32[]{:S(2)}) async-start(), calls=%async_computation.16 | async-start | bytes 1310720 | tf_op jit(solution)/shard_map/all_gather | solution.py:146
  54.6 54.7 %all-gather.51.cloned.1.call-start = ((), (), s32[]{:S(2)}) async-start(), calls=%async_computation.17 | async-start | bytes 1310720 | tf_op jit(solution)/shard_map/all_gather | solution.py:147
  59.1 92.4 %reduce-scatter.16.cloned.1.call-start = ((), (), s32[]{:S(2)}) async-start(), calls=%async_computation.18 | async-start | bytes 1310720 | tf_op jit(solution)/shard_map/reduce_scatter | solution.py:173
  124.0 60.7 %all-gather.53.cloned.1.call-start = ((), (), s32[]{:S(2)}) async-start(), calls=%async_computation.19 | async-start | bytes 1310720 | tf_op jit(solution)/shard_map/all_gather | solution.py:130
  156.7 72.6 %all-gather.55.cloned.1.call-start = ((), (), s32[]{:S(2)}) async-start(), calls=%async_computation.20 | async-start | bytes 1310720 | tf_op jit(solution)/shard_map/all_gather | solution.py:146
  203.4 54.1 %all-gather.57.cloned.1.call-start = ((), (), s32[]{:S(2)}) async-start(), calls=%async_computation.21 | async-start | bytes 1310720 | tf_op jit(solution)/shard_map/all_gather | solution.py:147
  210.9 90.9 %reduce-scatter.18.cloned.1.call-start = ((), (), s32[]{:S(2)}) async-start(), calls=%async_computation.22 | async-start | bytes 1310720 | tf_op jit(solution)/shard_map/reduce_scatter | solution.py:173
  274.4 61.5 %all-gather.59.cloned.1.call-start = ((), (), s32[]{:S(2)}) async-start(), calls=%async_computation.23 | async-start | bytes 1310720 | tf_op jit(solution)/shard_map/all_gather | solution.py:130
  307.9 72.6 %all-gather.61.cloned.1.call-start = ((), (), s32[]{:S(2)}) async-start(), calls=%async_computation.24 | async-start | bytes 1310720 | tf_op jit(solution)/shard_map/all_gather | solution.py:146
  354.6 54.2 %all-gather.63.cloned.1.call-start = ((), (), s32[]{:S(2)}) async-start(), calls=%async_computation.25 | async-start | bytes 1310720 | tf_op jit(solution)/shard_map/all_gather | solution.py:147
  358.2 94.8 %reduce-scatter.20.cloned.1.call-start = ((), (), s32[]{:S(2)}) async-start(), calls=%async_computation.26 | async-start | bytes 1310720 | tf_op jit(solution)/shard_map/reduce_scatter | solution.py:173
  425.6 61.5 %all-gather.65.cloned.1.call-start = ((), (), s32[]{:S(2)}) async-start(), calls=%async_computation.27 | async-start | bytes 1310720 | tf_op jit(solution)/shard_map/all_gather | solution.py:130
  459.1 72.5 %all-gather.67.cloned.1.call-start = ((), (), s32[]{:S(2)}) async-start(), calls=%async_computation.28 | async-start | bytes 1310720 | tf_op jit(solution)/shard_map/all_gather | solution.py:146
  509.4 79.8 %all-gather.97.cloned.1.call-start = ((), (), s32[]{:S(2)}) async-start(), calls=%async_computation.55 | async-start | bytes 1310720 | tf_op jit(solution)/shard_map/all_gather | solution.py:219
  511.7 106.8 %reduce-scatter.22.cloned.1.call-start = ((), (), s32[]{:S(2)}) async-start(), calls=%async_computation.30 | async-start | bytes 1310720 | tf_op jit(solution)/shard_map/reduce_scatter | solution.py:173
  576.7 75.9 %all-gather.71.cloned.1.call-start = ((), (), s32[]{:S(2)}) async-start(), calls=%async_computation.31 | async-start | bytes 1310720 | tf_op jit(solution)/shard_map/all_gather | solution.py:130
  625.6 85.4 %all-gather.73.cloned.1.call-start = ((), (), s32[]{:S(2)}) async-start(), calls=%async_computation.32 | async-start | bytes 1310720 | tf_op jit(solution)/shard_map/all_gather | solution.py:146
  685.2 68.3 %all-gather.95.cloned.1.call-start = ((), (), s32[]{:S(2)}) async-start(), calls=%async_computation.54 | async-start | bytes 1310720 | tf_op jit(solution)/shard_map/all_gather | solution.py:233
  697.6 84.1 %all-gather.99.cloned.1.call-start = ((), (), s32[]{:S(2)}) async-start(), calls=%async_computation.56 | async-start | bytes 1310720 | tf_op jit(solution)/shard_map/all_gather | solution.py:234
  709.0 117.8 %reduce-scatter.26.cloned.1.call-start = ((), (), s32[]{:S(2)}) async-start(), calls=%async_computation.35 | async-start | bytes 2621440 | tf_op jit(solution)/shard_map/reduce_scatter | solution.py:270
  791.4 88.6 %reduce-scatter.28.cloned.1.call-start = ((), (), s32[]{:S(2)}) async-start(), calls=%async_computation.36 | async-start | bytes 1310720 | tf_op jit(solution)/shard_map/reduce_scatter | solution.py:301
  852.6 54.2 %all-gather.101.cloned.1.call-start = ((), (), s32[]{:S(2)}) async-start(), calls=%async_computation.57 | async-start | bytes 1310720 | tf_op jit(solution)/shard_map/all_gather | solution.py:233
  853.3 82.9 %all-gather.77.cloned.1.call-start = ((), (), s32[]{:S(2)}) async-start(), calls=%async_computation.37 | async-start | bytes 1310720 | tf_op jit(solution)/shard_map/all_gather | solution.py:219
  891.3 72.3 %all-gather.103.cloned.1.call-start = ((), (), s32[]{:S(2)}) async-start(), calls=%async_computation.58 | async-start | bytes 1310720 | tf_op jit(solution)/shard_map/all_gather | solution.py:234
  891.9 116.8 %reduce-scatter.30.cloned.1.call-start = ((), (), s32[]{:S(2)}) async-start(), calls=%async_computation.38 | async-start | bytes 2621440 | tf_op jit(solution)/shard_map/reduce_scatter | solution.py:270
  973.3 88.6 %reduce-scatter.32.cloned.1.call-start = ((), (), s32[]{:S(2)}) async-start(), calls=%async_computation.39 | async-start | bytes 1310720 | tf_op jit(solution)/shard_map/reduce_scatter | solution.py:301
  1034.5 54.0 %all-gather.105.cloned.1.call-start = ((), (), s32[]{:S(2)}) async-start(), calls=%async_computation.59 | async-start | bytes 1310720 | tf_op jit(solution)/shard_map/all_gather | solution.py:233
  1035.1 83.0 %all-gather.79.cloned.1.call-start = ((), (), s32[]{:S(2)}) async-start(), calls=%async_computation.40 | async-start | bytes 1310720 | tf_op jit(solution)/shard_map/all_gather | solution.py:219
  1073.2 72.5 %all-gather.107.cloned.1.call-start = ((), (), s32[]{:S(2)}) async-start(), calls=%async_computation.60 | async-start | bytes 1310720 | tf_op jit(solution)/shard_map/all_gather | solution.py:234
  1074.0 116.9 %reduce-scatter.34.cloned.1.call-start = ((), (), s32[]{:S(2)}) async-start(), calls=%async_computation.41 | async-start | bytes 2621440 | tf_op jit(solution)/shard_map/reduce_scatter | solution.py:270
  1155.5 89.3 %reduce-scatter.36.cloned.1.call-start = ((), (), s32[]{:S(2)}) async-start(), calls=%async_computation.42 | async-start | bytes 1310720 | tf_op jit(solution)/shard_map/reduce_scatter | solution.py:301
  1217.3 54.2 %all-gather.109.cloned.1.call-start = ((), (), s32[]{:S(2)}) async-start(), calls=%async_computation.61 | async-start | bytes 1310720 | tf_op jit(solution)/shard_map/all_gather | solution.py:233
  1218.1 82.9 %all-gather.81.cloned.1.call-start = ((), (), s32[]{:S(2)}) async-start(), calls=%async_computation.43 | async-start | bytes 1310720 | tf_op jit(solution)/shard_map/all_gather | solution.py:219
  1254.6 73.8 %all-gather.111.cloned.1.call-start = ((), (), s32[]{:S(2)}) async-start(), calls=%async_computation.62 | async-start | bytes 1310720 | tf_op jit(solution)/shard_map/all_gather | solution.py:234
  1255.2 118.3 %reduce-scatter.38.cloned.1.call-start = ((), (), s32[]{:S(2)}) async-start(), calls=%async_computation.44 | async-start | bytes 2621440 | tf_op jit(solution)/shard_map/reduce_scatter | solution.py:270
  1338.2 89.3 %reduce-scatter.40.cloned.1.call-start = ((), (), s32[]{:S(2)}) async-start(), calls=%async_computation.45 | async-start | bytes 1310720 | tf_op jit(solution)/shard_map/reduce_scatter | solution.py:301
  1400.0 54.2 %all-gather.113.cloned.1.call-start = ((), (), s32[]{:S(2)}) async-start(), calls=%async_computation.63 | async-start | bytes 1310720 | tf_op jit(solution)/shard_map/all_gather | solution.py:233
  1400.7 83.0 %all-gather.83.cloned.1.call-start = ((), (), s32[]{:S(2)}) async-start(), calls=%async_computation.46 | async-start | bytes 1310720 | tf_op jit(solution)/shard_map/all_gather | solution.py:219
  1437.3 74.1 %all-gather.115.cloned.1.call-start = ((), (), s32[]{:S(2)}) async-start(), calls=%async_computation.64 | async-start | bytes 1310720 | tf_op jit(solution)/shard_map/all_gather | solution.py:234
  1438.0 142.5 %all-gather.87.cloned.1.call-start = ((), (), s32[]{:S(2)}) async-start(), calls=%async_computation.50 | async-start | bytes 1310720 | tf_op jit(solution)/shard_map/all_gather | solution.py:296
  1438.6 157.2 %all-gather.85.cloned.1.call-start = ((), (), s32[]{:S(2)}) async-start(), calls=%async_computation.49 | async-start | bytes 1310720 | tf_op jit(solution)/shard_map/all_gather | solution.py:296
  1439.3 180.3 %all-gather.89.cloned.1.call-start = ((), (), s32[]{:S(2)}) async-start(), calls=%async_computation.51 | async-start | bytes 1310720 | tf_op jit(solution)/shard_map/all_gather | solution.py:296
  1439.9 203.6 %all-gather.91.cloned.1.call-start = ((), (), s32[]{:S(2)}) async-start(), calls=%async_computation.52 | async-start | bytes 1310720 | tf_op jit(solution)/shard_map/all_gather | solution.py:296
  1460.2 231.3 %reduce-scatter.42.cloned.1.call-start = ((), (), s32[]{:S(2)}) async-start(), calls=%async_computation.47 | async-start | bytes 2621440 | tf_op jit(solution)/shard_map/reduce_scatter | solution.py:270
  1526.3 185.2 %all-gather.93.cloned.1.call-start = ((), (), s32[]{:S(2)}) async-start(), calls=%async_computation.53 | async-start | bytes 1310720 | tf_op jit(solution)/shard_map/all_gather | solution.py:296
  1544.1 204.9 %reduce-scatter.24.cloned.1.call-start = ((), (), s32[]{:S(2)}) async-start(), calls=%async_computation.34 | async-start | bytes 1310720 | tf_op jit(solution)/shard_map/reduce_scatter | solution.py:173
  1557.3 199.2 %reduce-scatter.44.cloned.1.call-start = ((), (), s32[]{:S(2)}) async-start(), calls=%async_computation.48 | async-start | bytes 1310720 | tf_op jit(solution)/shard_map/reduce_scatter | solution.py:301
  1711.4 493.2 %all-reduce.5.cloned.1.call-start = ((), (), s32[]{:S(2)}) async-start(), calls=%async_computation.65 | async-start | bytes 50331648 | tf_op jit(solution)/shard_map/psum | solution.py:328
  (193 other events, 8569.4 us)
Sparse Core Ops, SparseCore 0:
  13.0 30.6 all-gather.46
  54.7 25.7 all-gather.48
  82.9 26.3 all-gather.50
  124.1 27.2 reduce-scatter.15
  156.8 27.7 all-gather.52
  203.5 25.7 all-gather.54
  231.1 26.3 all-gather.56
  274.5 27.2 reduce-scatter.17
  308.0 27.7 all-gather.58
  354.7 25.7 all-gather.60
  382.3 26.3 all-gather.62
  425.7 27.2 reduce-scatter.19
  459.2 27.7 all-gather.64
  505.8 25.7 all-gather.66
  533.3 26.3 all-gather.68
  561.1 27.9 all-gather.96
  591.8 26.6 reduce-scatter.21
  625.7 26.8 all-gather.70
  671.4 25.7 all-gather.72
  698.9 26.3 all-gather.74
  727.1 26.3 all-gather.94
  755.3 26.3 all-gather.98
  791.5 35.1 reduce-scatter.25
  852.7 27.2 reduce-scatter.27
  908.2 27.9 all-gather.76
  937.9 25.7 all-gather.102
  973.4 35.1 reduce-scatter.29
  1034.6 27.2 reduce-scatter.31
  1090.1 27.9 all-gather.78
  1120.0 25.7 all-gather.106
  1155.6 35.1 reduce-scatter.33
  1217.5 27.2 reduce-scatter.35
  1272.9 27.9 all-gather.80
  1302.6 25.7 all-gather.110
  1338.3 35.1 reduce-scatter.37
  1400.1 27.2 reduce-scatter.39
  1429.3 24.8 all-gather.112
  1455.8 27.9 all-gather.82
  1485.6 25.7 all-gather.114
  1512.8 27.9 all-gather.86
  1542.4 27.3 all-gather.84
  1571.2 27.3 all-gather.88
  1600.0 27.3 all-gather.90
  1630.2 34.5 reduce-scatter.41
  1666.2 27.9 all-gather.92
  1696.4 26.6 reduce-scatter.23
  1726.0 25.7 reduce-scatter.43
  1756.0 448.6 all-reduce.4
  (3 shorter events, 74.4 us)
where the time goes:
time: 2310 us; the launch traced here: 2300 us
  waiting for transfers between devices  1210 us (52%)
  matrix products  482 us (21%)
  local copies, waits for them, and re-layouts  269 us (12%)
  other arithmetic  261 us (11%)
  blocking collectives  36.1 us (2%)
    psum x1, waiting for transfers between devices, on_device(): lax.psum(total_w_in.astype(jnp.bfloat16), 'ctx').astype(jnp.float32)  408 us
    all_gather x5, waiting for transfers between devices, on_device(): lax.all_gather(normed_b, 'tp', axis=0, tiled=True)  107 us
    reduce_scatter x5, waiting for transfers between devices, on_device(): lax.psum_scatter(lax.dot_general(grad_proj_b, w_in, contract_cols, prefer...  102 us
    reduce_scatter x5, waiting for transfers between devices, on_device(): lax.psum_scatter(jnp.dot(branch_in, w_out, preferred_element_type=jnp.flo...  101 us
    all_gather x5, waiting for transfers between devices, on_device(): fold_pieces = lax.all_gather(grad_out_b, 'tp', axis=0, tiled=True)  93.7 us
    dot_general x5, matrix products, on_device(): lax.dot_general(lax.all_gather(backward_normed_b, 'tp', axis=0, tiled=Tru...  93.2 us
    reduce_scatter x5, waiting for transfers between devices, on_device(): lax.psum_scatter(jnp.concatenate([grad_key_part, grad_value_part], axis=2...  86 us
    all_gather x5, waiting for transfers between devices, on_device(): values_part = lax.all_gather(values_b, 'ctx', axis=0, tiled=True)  85.2 us
  transfers between devices with their start and end apart: 59, of which 48 were waited for; matrix products, arithmetic and copies ran while one was open for 26% of the time, Pallas kernels for 0%

commit v1 on v0

--- a/solution.py
+++ b/solution.py
@@ -9,6 +9,12 @@
 NEGATIVE = -1e30
 GELU_ROOT = 0.7978845608028654
 GELU_CUBE = 0.044715
+
+
+def make_zone(u, link_axis):
+    reached = lax.all_gather(u, axis_name=link_axis)
+    wide_out = jnp.sum(reached, axis=0)
+    return wide_out
 
 
 def from_behind(x, axis, by):
@@ -325,7 +331,7 @@
         received = from_behind(grad_x_b, "section", -1)
     total_w_in, total_w_out, total_bias_in, total_gain, total_shift, total_bias_out = totals
     sum_w_in, sum_w_out, sum_bias_in, sum_gain, sum_shift, sum_bias_out = (
-        lax.psum(total_w_in.astype(jnp.bfloat16), "ctx").astype(jnp.float32),
+        make_zone(total_w_in.astype(jnp.bfloat16), "ctx").astype(jnp.float32),
         lax.psum(total_w_out.astype(jnp.bfloat16), "ctx").astype(jnp.float32),
         lax.psum(total_bias_in.astype(jnp.bfloat16), "ctx").astype(jnp.float32),
         lax.psum(total_gain.astype(jnp.bfloat16), "ctx").astype(jnp.float32),

time: 2310 us -> 2580 us (1.12)
  waiting for transfers between devices: 1210 us -> 1450 us
  other arithmetic: 261 us -> 294 us
    all_gather x0 -> x1, waiting for transfers between devices: none -> 468 us  [make_zone(): reached = lax.all_gather(u, axis_name=link_axis)]
    psum x1, waiting for transfers between devices: 408 us -> 171 us  [on_device(): lax.psum(total_w_out.astype(jnp.bfloat16), 'ctx').astype(jnp.float32)]
    reduce_sum x0 -> x1, other arithmetic: none -> 27.6 us  [make_zone(): wide_out = jnp.sum(reached, axis=0)]
    unnamed x367 -> x349, local copies, waits for them, and re-layouts: 64.8 us -> 65.4 us
  transfers between devices with their start and end apart: 59 -> 60, of which waited for: 48 -> 50; matrix products, arithmetic and copies ran while one was open for 26% -> 24% of each run, Pallas kernels for 0% -> 0%
where the time goes in v1:
time: 2580 us; the launch traced here: 2570 us
  waiting for transfers between devices  1450 us (56%)
  matrix products  485 us (19%)
  other arithmetic  294 us (11%)
  local copies, waits for them, and re-layouts  269 us (10%)
  blocking collectives  34.3 us (1%)
    all_gather x1, waiting for transfers between devices, make_zone(): reached = lax.all_gather(u, axis_name=link_axis)  468 us
    psum x1, waiting for transfers between devices, on_device(): lax.psum(total_w_out.astype(jnp.bfloat16), 'ctx').astype(jnp.float32)  171 us
    reduce_scatter x5, waiting for transfers between devices, on_device(): lax.psum_scatter(lax.dot_general(grad_proj_b, w_in, contract_cols, prefer...  108 us
    all_gather x5, waiting for transfers between devices, on_device(): lax.all_gather(normed_b, 'tp', axis=0, tiled=True)  107 us
    reduce_scatter x5, waiting for transfers between devices, on_device(): lax.psum_scatter(jnp.dot(branch_in, w_out, preferred_element_type=jnp.flo...  101 us
    dot_general x5, matrix products, on_device(): lax.dot_general(lax.all_gather(backward_normed_b, 'tp', axis=0, tiled=Tru...  96.8 us
    all_gather x5, waiting for transfers between devices, on_device(): fold_pieces = lax.all_gather(grad_out_b, 'tp', axis=0, tiled=True)  94.1 us
    reduce_scatter x5, waiting for transfers between devices, on_device(): lax.psum_scatter(jnp.concatenate([grad_key_part, grad_value_part], axis=2...  86.2 us
  transfers between devices with their start and end apart: 60, of which 50 were waited for; matrix products, arithmetic and copies ran while one was open for 24% of the time, Pallas kernels for 0%

profile of v1, /device:TPU:0, one launch (start us, length us, event | category | flops | bytes accessed | tf_op | source)
XLA Modules:
  0.0 2569.4 jit_solution(2942703494254616139)
XLA Ops:
  61.6 18.9 all-gather.51.cloned.1.call-done
  89.4 19.9 all-gather.53.cloned.1.call-done
  124.1 27.4 %reduce-scatter.16.cloned.1.call-done = bf16[64,2048]{1,0:T(8,128)(2,1)} async-done(((bf16[256,2048]{1,0:T(8,128)(2,1)}), bf16[64,2048]{1,0:T(8,128)(2,1)}) %reduce-scatter.16.cloned.1.call-update) | async-done | bytes 262160 | tf_op jit(solution)/shard_map/reduce_scatter | solution.py:179
  156.8 27.9 %all-gather.55.cloned.1.call-done = bf16[256,2048]{1,0:T(8,128)(2,1)} async-done(((bf16[64,2048]{1,0:T(8,128)(2,1)}), bf16[256,2048]{1,0:T(8,128)(2,1)}) %all-gather.55.cloned.1.call-update) | async-done | bytes 1048592 | tf_op jit(solution)/shard_map/all_gather | solution.py:136
  215.8 13.5 all-gather.57.cloned.1.call-done
  238.3 19.2 all-gather.59.cloned.1.call-done
  275.1 26.7 %reduce-scatter.18.cloned.1.call-done = bf16[64,2048]{1,0:T(8,128)(2,1)} async-done(((bf16[256,2048]{1,0:T(8,128)(2,1)}), bf16[64,2048]{1,0:T(8,128)(2,1)}) %reduce-scatter.18.cloned.1.call-update) | async-done | bytes 262160 | tf_op jit(solution)/shard_map/reduce_scatter | solution.py:179
  308.3 27.5 %all-gather.61.cloned.1.call-done = bf16[256,2048]{1,0:T(8,128)(2,1)} async-done(((bf16[64,2048]{1,0:T(8,128)(2,1)}), bf16[256,2048]{1,0:T(8,128)(2,1)}) %all-gather.61.cloned.1.call-update) | async-done | bytes 1048592 | tf_op jit(solution)/shard_map/all_gather | solution.py:136
  363.2 17.4 all-gather.63.cloned.1.call-done
  389.6 19.2 all-gather.65.cloned.1.call-done
  426.4 26.7 %reduce-scatter.20.cloned.1.call-done = bf16[64,2048]{1,0:T(8,128)(2,1)} async-done(((bf16[256,2048]{1,0:T(8,128)(2,1)}), bf16[64,2048]{1,0:T(8,128)(2,1)}) %reduce-scatter.20.cloned.1.call-update) | async-done | bytes 262160 | tf_op jit(solution)/shard_map/reduce_scatter | solution.py:179
  459.4 27.7 %all-gather.67.cloned.1.call-done = bf16[256,2048]{1,0:T(8,128)(2,1)} async-done(((bf16[64,2048]{1,0:T(8,128)(2,1)}), bf16[256,2048]{1,0:T(8,128)(2,1)}) %all-gather.67.cloned.1.call-update) | async-done | bytes 1048592 | tf_op jit(solution)/shard_map/all_gather | solution.py:136
  516.7 14.9 all-gather.69.cloned.1.call-done
  540.7 19.0 all-gather.71.cloned.1.call-done
  598.6 20.0 reduce-scatter.22.cloned.1.call-done
  732.7 20.9 all-gather.97.cloned.1.call-done
  762.6 19.2 all-gather.101.cloned.1.call-done
  853.4 26.6 %reduce-scatter.28.cloned.1.call-done = bf16[64,2048]{1,0:T(8,128)(2,1)} async-done(((bf16[256,2048]{1,0:T(8,128)(2,1)}), bf16[64,2048]{1,0:T(8,128)(2,1)}) %reduce-scatter.28.cloned.1.call-update) | async-done | bytes 262160 | tf_op jit(solution)/shard_map/reduce_scatter | solution.py:307
  892.2 14.6 all-gather.103.cloned.1.call-done
  912.8 23.4 all-gather.79.cloned.1.call-done
  983.4 25.3 reduce-scatter.30.cloned.1.call-done
  1037.0 25.0 reduce-scatter.32.cloned.1.call-done
  1074.5 14.1 all-gather.107.cloned.1.call-done
  1094.6 23.6 all-gather.81.cloned.1.call-done
  1165.5 25.3 reduce-scatter.34.cloned.1.call-done
  1218.4 25.7 reduce-scatter.36.cloned.1.call-done
  1254.7 16.1 all-gather.111.cloned.1.call-done
  1276.9 23.4 all-gather.83.cloned.1.call-done
  1347.4 25.3 reduce-scatter.38.cloned.1.call-done
  1400.4 25.7 reduce-scatter.40.cloned.1.call-done
  1437.1 15.7 all-gather.115.cloned.1.call-done
  1458.8 23.6 all-gather.85.cloned.1.call-done
  1496.0 14.0 all-gather.117.cloned.1.call-done
  1617.6 26.1 %add_convert_fusion.1 = bf16[2560,2048]{1,0:T(8,128)(2,1)} fusion(f32[2560,2048]{1,0:T(8,128)} %fusion.191, f32[2560,2048]{1,0:T(8,128)} %fusion.193, f32[2560,2048]{1,0:T(8,128)} %fusion.195, f32[2560,2048]{1,0:T(8,128)} %fusion.197, bf16[256,2048]{1,0:T(8,128)(2,1)S(1)} %copy-done.86, pred[]{:T(512)S(6)} %and.120, pred[]{:T(512)S(6)} %and.118, ...), kind=kOutput, calls=%fused_computation.1 | convolution fusion | flops 2736783360 | bytes 96731144 | tf_op jit(solution)/shard_map/dot_general | solution.py:226
  1645.0 15.2 fusion.526
  1660.2 15.1 fusion.527
  1675.3 15.6 fusion.525
  1690.9 15.7 fusion.524
  1706.7 35.2 %add_convert_fusion = bf16[2048,3584]{1,0:T(8,128)(2,1)} fusion(f32[2048,3584]{1,0:T(8,128)} %fusion.524, f32[2048,3584]{1,0:T(8,128)} %fusion.525, f32[2048,3584]{1,0:T(8,128)} %fusion.526, f32[2048,3584]{1,0:T(8,128)} %fusion.527, bf16[256,2048]{1,0:T(8,128)(2,1)} %all-gather.95.cloned.1.call-done, pred[]{:T(512)S(6)} %and.120, pred[]{:T(512)S(6)} %and.118, ...), kind=kOutput, calls=%fused_computation | convolution fusion | flops 3838836736 | bytes 135004160 | tf_op jit(solution)/shard_map/dot_general | solution.py:301
  1758.6 17.0 all-reduce.1
  1776.8 17.3 all-reduce
  1795.5 171.1 %all-reduce.4.cloned.1.call-done = bf16[2560,2048]{1,0:T(8,128)(2,1)} async-done(((bf16[2560,2048]{1,0:T(8,128)(2,1)}), bf16[2560,2048]{1,0:T(8,128)(2,1)}) %all-reduce.4.cloned.1.call-update) | async-done | bytes 10485776 | tf_op jit(solution)/shard_map/psum | solution.py:335
  1966.6 20.2 convert_element_type.737
  1993.2 15.3 slice_bitcast_fusion
  2008.4 468.1 %all-gather.119.cloned.1.call-done = bf16[8192,3584]{1,0:T(8,128)(2,1)} async-done(((bf16[2048,3584]{1,0:T(8,128)(2,1)}), bf16[8192,3584]{1,0:T(8,128)(2,1)}) %all-gather.119.cloned.1.call-update) | async-done | bytes 58720272 | tf_op jit(solution)/shard_map/all_gather | solution.py:15
  2476.6 27.6 %reduce_sum.602 = bf16[2048,3584]{1,0:T(8,128)(2,1)} reduce(bf16[4,2048,3584]{2,1,0:T(8,128)(2,1)} %bitcast.819, bf16[]{:T(256)} %constant.538.clone.1), dimensions={0}, to_apply=%region_74.75 | reduce | flops 22020096 | bytes 73400320 | tf_op jit(solution)/shard_map/reduce_sum | solution.py:16
  2525.7 12.6 copy.196
  2538.3 12.6 copy.202
  (876 shorter events, 953.9 us)
Async XLA Ops:
  12.8 67.7 %all-gather.51.cloned.1.call-start = ((), (), s32[]{:S(2)}) async-start(), calls=%async_computation.16 | async-start | bytes 1310720 | tf_op jit(solution)/shard_map/all_gather | solution.py:152
  54.6 54.7 %all-gather.53.cloned.1.call-start = ((), (), s32[]{:S(2)}) async-start(), calls=%async_computation.17 | async-start | bytes 1310720 | tf_op jit(solution)/shard_map/all_gather | solution.py:153
  59.1 92.4 %reduce-scatter.16.cloned.1.call-start = ((), (), s32[]{:S(2)}) async-start(), calls=%async_computation.18 | async-start | bytes 1310720 | tf_op jit(solution)/shard_map/reduce_scatter | solution.py:179
  124.0 60.6 %all-gather.55.cloned.1.call-start = ((), (), s32[]{:S(2)}) async-start(), calls=%async_computation.19 | async-start | bytes 1310720 | tf_op jit(solution)/shard_map/all_gather | solution.py:136
  156.7 72.6 %all-gather.57.cloned.1.call-start = ((), (), s32[]{:S(2)}) async-start(), calls=%async_computation.20 | async-start | bytes 1310720 | tf_op jit(solution)/shard_map/all_gather | solution.py:152
  203.4 54.1 %all-gather.59.cloned.1.call-start = ((), (), s32[]{:S(2)}) async-start(), calls=%async_computation.21 | async-start | bytes 1310720 | tf_op jit(solution)/shard_map/all_gather | solution.py:153
  210.9 90.9 %reduce-scatter.18.cloned.1.call-start = ((), (), s32[]{:S(2)}) async-start(), calls=%async_computation.22 | async-start | bytes 1310720 | tf_op jit(solution)/shard_map/reduce_scatter | solution.py:179
  274.3 61.5 %all-gather.61.cloned.1.call-start = ((), (), s32[]{:S(2)}) async-start(), calls=%async_computation.23 | async-start | bytes 1310720 | tf_op jit(solution)/shard_map/all_gather | solution.py:136
  307.9 72.6 %all-gather.63.cloned.1.call-start = ((), (), s32[]{:S(2)}) async-start(), calls=%async_computation.24 | async-start | bytes 1310720 | tf_op jit(solution)/shard_map/all_gather | solution.py:152
  354.6 54.2 %all-gather.65.cloned.1.call-start = ((), (), s32[]{:S(2)}) async-start(), calls=%async_computation.25 | async-start | bytes 1310720 | tf_op jit(solution)/shard_map/all_gather | solution.py:153
  358.3 94.8 %reduce-scatter.20.cloned.1.call-start = ((), (), s32[]{:S(2)}) async-start(), calls=%async_computation.26 | async-start | bytes 1310720 | tf_op jit(solution)/shard_map/reduce_scatter | solution.py:179
  425.6 61.5 %all-gather.67.cloned.1.call-start = ((), (), s32[]{:S(2)}) async-start(), calls=%async_computation.27 | async-start | bytes 1310720 | tf_op jit(solution)/shard_map/all_gather | solution.py:136
  459.2 72.4 %all-gather.69.cloned.1.call-start = ((), (), s32[]{:S(2)}) async-start(), calls=%async_computation.28 | async-start | bytes 1310720 | tf_op jit(solution)/shard_map/all_gather | solution.py:152
  509.4 79.7 %all-gather.99.cloned.1.call-start = ((), (), s32[]{:S(2)}) async-start(), calls=%async_computation.56 | async-start | bytes 1310720 | tf_op jit(solution)/shard_map/all_gather | solution.py:225
  511.8 106.8 %reduce-scatter.22.cloned.1.call-start = ((), (), s32[]{:S(2)}) async-start(), calls=%async_computation.30 | async-start | bytes 1310720 | tf_op jit(solution)/shard_map/reduce_scatter | solution.py:179
  576.6 76.0 %all-gather.73.cloned.1.call-start = ((), (), s32[]{:S(2)}) async-start(), calls=%async_computation.31 | async-start | bytes 1310720 | tf_op jit(solution)/shard_map/all_gather | solution.py:136
  625.6 85.8 %all-gather.75.cloned.1.call-start = ((), (), s32[]{:S(2)}) async-start(), calls=%async_computation.32 | async-start | bytes 1310720 | tf_op jit(solution)/shard_map/all_gather | solution.py:152
  685.3 68.3 %all-gather.97.cloned.1.call-start = ((), (), s32[]{:S(2)}) async-start(), calls=%async_computation.55 | async-start | bytes 1310720 | tf_op jit(solution)/shard_map/all_gather | solution.py:239
  697.8 84.0 %all-gather.101.cloned.1.call-start = ((), (), s32[]{:S(2)}) async-start(), calls=%async_computation.57 | async-start | bytes 1310720 | tf_op jit(solution)/shard_map/all_gather | solution.py:240
  709.2 117.6 %reduce-scatter.26.cloned.1.call-start = ((), (), s32[]{:S(2)}) async-start(), calls=%async_computation.35 | async-start | bytes 2621440 | tf_op jit(solution)/shard_map/reduce_scatter | solution.py:276
  791.5 88.6 %reduce-scatter.28.cloned.1.call-start = ((), (), s32[]{:S(2)}) async-start(), calls=%async_computation.36 | async-start | bytes 1310720 | tf_op jit(solution)/shard_map/reduce_scatter | solution.py:307
  852.6 54.2 %all-gather.103.cloned.1.call-start = ((), (), s32[]{:S(2)}) async-start(), calls=%async_computation.58 | async-start | bytes 1310720 | tf_op jit(solution)/shard_map/all_gather | solution.py:239
  853.4 82.9 %all-gather.79.cloned.1.call-start = ((), (), s32[]{:S(2)}) async-start(), calls=%async_computation.37 | async-start | bytes 1310720 | tf_op jit(solution)/shard_map/all_gather | solution.py:225
  891.3 72.4 %all-gather.105.cloned.1.call-start = ((), (), s32[]{:S(2)}) async-start(), calls=%async_computation.59 | async-start | bytes 1310720 | tf_op jit(solution)/shard_map/all_gather | solution.py:240
  891.9 116.8 %reduce-scatter.30.cloned.1.call-start = ((), (), s32[]{:S(2)}) async-start(), calls=%async_computation.38 | async-start | bytes 2621440 | tf_op jit(solution)/shard_map/reduce_scatter | solution.py:276
  973.4 88.7 %reduce-scatter.32.cloned.1.call-start = ((), (), s32[]{:S(2)}) async-start(), calls=%async_computation.39 | async-start | bytes 1310720 | tf_op jit(solution)/shard_map/reduce_scatter | solution.py:307
  1035.2 83.0 %all-gather.81.cloned.1.call-start = ((), (), s32[]{:S(2)}) async-start(), calls=%async_computation.40 | async-start | bytes 1310720 | tf_op jit(solution)/shard_map/all_gather | solution.py:225
  1073.2 72.6 %all-gather.109.cloned.1.call-start = ((), (), s32[]{:S(2)}) async-start(), calls=%async_computation.61 | async-start | bytes 1310720 | tf_op jit(solution)/shard_map/all_gather | solution.py:240
  1074.0 116.8 %reduce-scatter.34.cloned.1.call-start = ((), (), s32[]{:S(2)}) async-start(), calls=%async_computation.41 | async-start | bytes 2621440 | tf_op jit(solution)/shard_map/reduce_scatter | solution.py:276
  1155.5 88.7 %reduce-scatter.36.cloned.1.call-start = ((), (), s32[]{:S(2)}) async-start(), calls=%async_computation.42 | async-start | bytes 1310720 | tf_op jit(solution)/shard_map/reduce_scatter | solution.py:307
  1216.7 54.2 %all-gather.111.cloned.1.call-start = ((), (), s32[]{:S(2)}) async-start(), calls=%async_computation.62 | async-start | bytes 1310720 | tf_op jit(solution)/shard_map/all_gather | solution.py:239
  1217.4 82.9 %all-gather.83.cloned.1.call-start = ((), (), s32[]{:S(2)}) async-start(), calls=%async_computation.43 | async-start | bytes 1310720 | tf_op jit(solution)/shard_map/all_gather | solution.py:225
  1253.9 73.9 %all-gather.113.cloned.1.call-start = ((), (), s32[]{:S(2)}) async-start(), calls=%async_computation.63 | async-start | bytes 1310720 | tf_op jit(solution)/shard_map/all_gather | solution.py:240
  1254.5 118.3 %reduce-scatter.38.cloned.1.call-start = ((), (), s32[]{:S(2)}) async-start(), calls=%async_computation.44 | async-start | bytes 2621440 | tf_op jit(solution)/shard_map/reduce_scatter | solution.py:276
  1337.4 88.6 %reduce-scatter.40.cloned.1.call-start = ((), (), s32[]{:S(2)}) async-start(), calls=%async_computation.45 | async-start | bytes 1310720 | tf_op jit(solution)/shard_map/reduce_scatter | solution.py:307
  1398.6 54.2 %all-gather.115.cloned.1.call-start = ((), (), s32[]{:S(2)}) async-start(), calls=%async_computation.64 | async-start | bytes 1310720 | tf_op jit(solution)/shard_map/all_gather | solution.py:239
  1399.4 83.0 %all-gather.85.cloned.1.call-start = ((), (), s32[]{:S(2)}) async-start(), calls=%async_computation.46 | async-start | bytes 1310720 | tf_op jit(solution)/shard_map/all_gather | solution.py:225
  1435.9 74.2 %all-gather.117.cloned.1.call-start = ((), (), s32[]{:S(2)}) async-start(), calls=%async_computation.65 | async-start | bytes 1310720 | tf_op jit(solution)/shard_map/all_gather | solution.py:240
  1436.6 165.5 %reduce-scatter.42.cloned.1.call-start = ((), (), s32[]{:S(2)}) async-start(), calls=%async_computation.47 | async-start | bytes 2621440 | tf_op jit(solution)/shard_map/reduce_scatter | solution.py:276
  1519.4 124.9 %all-gather.89.cloned.1.call-start = ((), (), s32[]{:S(2)}) async-start(), calls=%async_computation.50 | async-start | bytes 1310720 | tf_op jit(solution)/shard_map/all_gather | solution.py:302
  1520.1 140.1 %all-gather.87.cloned.1.call-start = ((), (), s32[]{:S(2)}) async-start(), calls=%async_computation.49 | async-start | bytes 1310720 | tf_op jit(solution)/shard_map/all_gather | solution.py:302
  1520.7 154.6 %all-gather.91.cloned.1.call-start = ((), (), s32[]{:S(2)}) async-start(), calls=%async_computation.51 | async-start | bytes 1310720 | tf_op jit(solution)/shard_map/all_gather | solution.py:302
  1521.3 169.6 %all-gather.93.cloned.1.call-start = ((), (), s32[]{:S(2)}) async-start(), calls=%async_computation.52 | async-start | bytes 1310720 | tf_op jit(solution)/shard_map/all_gather | solution.py:302
  1531.7 175.0 %all-gather.95.cloned.1.call-start = ((), (), s32[]{:S(2)}) async-start(), calls=%async_computation.53 | async-start | bytes 1310720 | tf_op jit(solution)/shard_map/all_gather | solution.py:302
  1541.0 203.2 %reduce-scatter.24.cloned.1.call-start = ((), (), s32[]{:S(2)}) async-start(), calls=%async_computation.34 | async-start | bytes 1310720 | tf_op jit(solution)/shard_map/reduce_scatter | solution.py:179
  1553.7 203.3 %reduce-scatter.44.cloned.1.call-start = ((), (), s32[]{:S(2)}) async-start(), calls=%async_computation.48 | async-start | bytes 1310720 | tf_op jit(solution)/shard_map/reduce_scatter | solution.py:307
  1617.6 349.0 %all-reduce.4.cloned.1.call-start = ((), (), s32[]{:S(2)}) async-start(), calls=%async_computation.54 | async-start | bytes 20971520 | tf_op jit(solution)/shard_map/psum | solution.py:335
  1643.8 832.7 %all-gather.119.cloned.1.call-start = ((), (), s32[]{:S(2)}) async-start(), calls=%async_computation.66 | async-start | bytes 73400320 | tf_op jit(solution)/shard_map/all_gather | solution.py:15
  (185 other events, 5110.0 us)
Sparse Core Ops, SparseCore 0:
  13.0 30.6 all-gather.48
  54.7 25.7 all-gather.50
  82.9 26.3 all-gather.52
  124.1 27.2 reduce-scatter.15
  156.8 27.7 all-gather.54
  203.5 25.7 all-gather.56
  231.1 26.3 all-gather.58
  274.4 27.2 reduce-scatter.17
  308.0 27.7 all-gather.60
  354.8 25.7 all-gather.62
  382.4 26.3 all-gather.64
  425.8 27.2 reduce-scatter.19
  459.3 27.7 all-gather.66
  505.9 25.7 all-gather.68
  533.3 26.3 all-gather.70
  561.1 27.9 all-gather.98
  591.8 26.6 reduce-scatter.21
  625.7 26.8 all-gather.72
  671.5 25.7 all-gather.74
  699.0 26.3 all-gather.76
  727.2 26.3 all-gather.96
  755.4 26.3 all-gather.100
  791.6 35.1 reduce-scatter.25
  852.8 27.2 reduce-scatter.27
  908.2 27.9 all-gather.78
  937.9 25.7 all-gather.104
  973.5 35.1 reduce-scatter.29
  1034.7 27.2 reduce-scatter.31
  1090.2 27.9 all-gather.80
  1120.0 25.7 all-gather.108
  1155.6 35.1 reduce-scatter.33
  1216.8 27.3 reduce-scatter.35
  1272.3 27.9 all-gather.82
  1302.0 25.7 all-gather.112
  1337.6 35.1 reduce-scatter.37
  1398.8 27.2 reduce-scatter.39
  1454.4 27.9 all-gather.84
  1484.2 25.7 all-gather.116
  1519.5 35.1 reduce-scatter.41
  1556.3 27.9 all-gather.88
  1585.7 27.3 all-gather.86
  1614.5 27.3 all-gather.90
  1643.4 27.3 all-gather.92
  1672.2 27.3 all-gather.94
  1701.7 26.6 reduce-scatter.23
  1731.3 25.7 reduce-scatter.43
  1761.0 205.5 all-reduce.3
  1969.0 507.4 all-gather.118
  (4 shorter events, 99.2 us)
